TPU v7x, 512 devices: a whole 4x8x8 slice. The times are simulated.
512 devices in a mesh: member: 16 (over z, core), band: 32 (over y, x).
Axes of the slice: x: 4, y: 8, z: 8, core: 2. Of those that a mesh axis runs over, the one named last changes fastest.
Arguments:
- ensemble: bfloat16 [16, 2, 16, 128, 1440], P('member', None, None, 'band'), may hold values from -6 to 6
- member_weight: float32 [16], replicated, may hold values from 0.5 to 2
- member_of_slot: int32 [16], P('member'), may hold values from 0 to 15, each once
- halfwidth: int32 [16], replicated, may hold values from 1 to 4, as said below
- static_root: float32 [16, 16], replicated, may hold values from -1.5 to 1.5
- innovation: bfloat16 [2, 16, 128, 1440], P(None, None, 'band'), may hold values from -6 to 6
- precision: bfloat16 [16, 128, 1440], P(None, 'band'), may hold values from 0.1 to 3
Outputs:
- control_members: float32 [16, 16, 128, 1440], P('member', None, 'band')
- control_static: float32 [16, 128, 1440], P(None, 'band')
- increment: float32 [2, 16, 128, 1440], P(None, 'member', 'band')
Inputs may be any that keep to these rules, and one draw needn't show every extreme that they name: `member_of_slot`: each member appears in exactly one slot. `halfwidth`: some level has a half-width of exactly 4.
All inputs are finite; a program needn't handle non-finite values.
Results may differ from a plain program's by a relative error of at most 0.0062.
Values may be sent and summed in bfloat16 or wider, within the bound.
A program may use at most 64 MiB of HBM per device.

v0:
```python
import math
import jax
import jax.numpy as jnp
from jax import lax
from jax.sharding import PartitionSpec as P

ITERS = 2
HMAX = 4
LREACH = 18
ensemble_share = 0.8
static_share = 0.6
length_scale = 6.0


def with_halo(block, sides, width):
    for axis, dim in sides:
        count = lax.axis_size(axis)
        forward = [(i, i + 1) for i in range(count - 1)]
        backward = [(target, source) for source, target in forward]
        low = lax.ppermute(
            lax.slice_in_dim(block, block.shape[dim] - width, None, axis=dim), axis, forward
        )
        high = lax.ppermute(lax.slice_in_dim(block, 0, width, axis=dim), axis, backward)
        block = jnp.concatenate([low, block, high], axis=dim)
    return block


def lon_kernel(reach, width):
    rows_index = jnp.arange(width + 2 * reach, dtype=jnp.int32)[:, None]
    cols_index = jnp.arange(width, dtype=jnp.int32)[None, :]
    distance = jnp.abs(rows_index - reach - cols_index).astype(jnp.float32)
    values = jnp.exp(-0.5 * (distance / length_scale) ** 2) / (
        length_scale * math.sqrt(2.0 * math.pi)
    )
    return jnp.where(distance <= reach, values, jnp.zeros_like(values)).astype(jnp.bfloat16)


def smooth_longitude(field, reach, blocks):
    width = field.shape[-1] // blocks
    pieces = field.reshape(field.shape[:-1] + (blocks, width))
    before = jnp.roll(pieces, 1, axis=-2)[..., width - reach :]
    after = jnp.roll(pieces, -1, axis=-2)[..., :reach]
    window = jnp.concatenate([before, pieces, after], axis=-1)
    kernel = lon_kernel(reach, width)
    result = jnp.einsum("...bm,mo->...bo", window, kernel, preferred_element_type=jnp.float32)
    return result.reshape(field.shape).astype(jnp.bfloat16)


def taper_weights(halfwidth, reach):
    offsets = jnp.abs(jnp.arange(-reach, reach + 1, dtype=jnp.int32)).astype(jnp.float32)
    spans = halfwidth.astype(jnp.float32)[:, None] + 1.0
    return jnp.maximum(1.0 - offsets[None, :] / spans, 0.0) / spans


def localize(field, taper):
    smoothed = smooth_longitude(field.astype(jnp.bfloat16), LREACH, 3)
    padded = with_halo(smoothed, (("band", 2),), HMAX)
    row_count = field.shape[2]
    summed = jnp.zeros(field.shape, jnp.float32)
    for offset in range(2 * HMAX + 1):
        summed = summed + taper[:, offset][None, :, None, None] * padded[
            :, :, offset : offset + row_count, :
        ].astype(jnp.float32)
    return summed


def local_dot(first_members, second_members, first_static, second_static, groups):
    return jnp.sum(first_members * second_members) + jnp.sum(first_static * second_static) / groups


def shards(ensemble, member_weight, member_of_slot, halfwidth, static_root, innovation, precision):
    member_count = member_weight.shape[0]
    picker = (member_of_slot[:, None] == jnp.arange(member_count, dtype=jnp.int32)[None, :]).astype(
        jnp.float32
    )
    scaled = jnp.sum(picker * member_weight[None, :], axis=1)
    taper = taper_weights(halfwidth, HMAX)
    precise = precision.astype(jnp.float32)
    groups = lax.axis_size("member")
    level_share = precision.shape[0] // groups
    first_level = lax.axis_index("member") * level_share

    def adjoint(weighted):
        folded = scaled[:, None, None, None] * jnp.sum(
            ensemble.astype(jnp.float32) * weighted[None], axis=1
        )
        grad_members = ensemble_share * localize(folded, taper)
        grad_static = static_share * jnp.einsum(
            "ql,qyx->lyx", static_root, jnp.sum(weighted, axis=0), precision=lax.Precision.HIGHEST
        )
        return (grad_members, grad_static)

    res_members, res_static = adjoint(precise[None] * innovation.astype(jnp.float32))
    dir_members, dir_static = (res_members, res_static)
    sol_members = jnp.zeros_like(res_members)
    sol_static = jnp.zeros_like(res_static)
    increment = jnp.zeros((), jnp.float32)
    norm_now = lax.psum(
        local_dot(res_members, res_members, res_static, res_static, groups), ("member", "band")
    )
    for iteration in range(ITERS):
        localized = localize(dir_members, taper)
        partial_image = ensemble_share * jnp.sum(
            scaled[:, None, None, None, None] * ensemble.astype(jnp.float32) * localized[:, None],
            axis=0,
        )
        summed = lax.psum(partial_image, "member")
        static = jnp.einsum("lq,qyx->lyx", static_root, dir_static, precision=lax.Precision.HIGHEST)
        image = summed + static_share * static[None]
        hessian_weighted = precise[None] * image
        hessian_grad_members, hessian_grad_static = adjoint(hessian_weighted)
        hes_members, hes_static, image = (
            dir_members + hessian_grad_members,
            dir_static + hessian_grad_static,
            image,
        )
        curvature = lax.psum(
            local_dot(dir_members, hes_members, dir_static, hes_static, groups), ("member", "band")
        )
        alpha = norm_now / curvature
        sol_members = sol_members + alpha * dir_members
        sol_static = sol_static + alpha * dir_static
        increment = increment + alpha * image
        res_members = res_members - alpha * hes_members
        res_static = res_static - alpha * hes_static
        if iteration + 1 < ITERS:
            norm_next = lax.psum(
                local_dot(res_members, res_members, res_static, res_static, groups),
                ("member", "band"),
            )
            ratio = norm_next / norm_now
            dir_members = res_members + ratio * dir_members
            dir_static = res_static + ratio * dir_static
            norm_now = norm_next
    increment = lax.dynamic_slice_in_dim(increment, first_level, level_share, 1)
    return (sol_members, sol_static, increment)


def solution(mesh):
    return jax.shard_map(
        shards,
        mesh=mesh,
        in_specs=(
            P("member", None, None, "band", None),
            P(),
            P("member"),
            P(),
            P(),
            P(None, None, "band", None),
            P(None, "band", None),
        ),
        out_specs=(
            P("member", None, "band", None),
            P(None, "band", None),
            P(None, "member", "band", None),
        ),
        check_vma=False,
    )
```

profile of v0, /device:TPU:1, one launch (start us, length us, event | category | flops | bytes accessed | tf_op | source)
XLA Modules:
  0.0 658.5 jit_solution(16516160532751708579)
XLA Ops:
  8.9 1.3 fusion.100
  10.1 1.6 fusion.13
  14.2 4.0 collective-permute-start
  18.2 1.3 collective-permute-start.1
  20.8 3.8 collective-permute-done.1
  26.7 4.0 collective-permute-start.2
  31.0 1.3 collective-permute-start.3
  33.3 4.1 collective-permute-done.3
  38.1 1.8 fusion.10
  41.3 126.7 %all-reduce.4.cloned.1.call-done = f32[2,16,4,1440]{3,2,1,0:T(4,128)} async-done(((f32[2,16,4,1440]{3,2,1,0:T(4,128)}), f32[2,16,4,1440]{3,2,1,0:T(4,128)}) %all-reduce.4.cloned.1.call-update) | async-done | bytes 737296 | tf_op jit(solution)/shard_map/psum | solution.py:107
  168.0 1.7 multiply_reduce_fusion.1
  172.6 3.1 collective-permute-start.4
  175.7 1.3 collective-permute-start.5
  177.0 1.4 fusion.42
  179.7 3.3 collective-permute-done.5
  184.0 2.1 multiply_reduce_fusion.4
  187.4 101.5 %all-reduce = (f32[]{:T(128)}, f32[]{:T(128)}) all-reduce(f32[]{:T(128)S(6)} %add.217, f32[]{:T(128)S(6)} %add.238), channel_id=1, replica_groups=mesh['member'=16,'band'=32] {'member','band'}, use_global_device_ids=true, to_apply=%region_5.6 | all-reduce | flops 2 | bytes 16 | tf_op jit(solution)/shard_map/psum | solution.py:98
  292.7 94.9 %psum.45 = f32[]{:T(128)} all-reduce(f32[]{:T(128)S(6)} %add.239), channel_id=1, replica_groups=mesh['member'=16,'band'=32] {'member','band'}, use_global_device_ids=true, to_apply=%region_14.15 | all-reduce | flops 1 | bytes 8 | tf_op jit(solution)/shard_map/psum | solution.py:127
  394.0 3.7 collective-permute-start.6
  397.7 1.3 collective-permute-start.7
  399.0 2.2 collective-permute-done.6
  401.3 3.8 collective-permute-done.7
  405.8 1.8 fusion.12
  409.1 116.4 %all-reduce.6.cloned.1.call-done = f32[2,16,4,1440]{3,2,1,0:T(4,128)} async-done(((f32[2,16,4,1440]{3,2,1,0:T(4,128)}), f32[2,16,4,1440]{3,2,1,0:T(4,128)}) %all-reduce.6.cloned.1.call-update) | async-done | bytes 737296 | tf_op jit(solution)/shard_map/psum | solution.py:107
  525.5 1.8 multiply_reduce_fusion
  531.2 3.1 collective-permute-start.8
  534.3 1.3 collective-permute-start.9
  535.6 1.2 fusion.17
  537.8 3.9 collective-permute-done.9
  542.7 2.0 fusion.39
  545.3 101.3 %psum.47 = f32[]{:T(128)} all-reduce(f32[]{:T(128)S(6)} %add.262), channel_id=1, replica_groups=mesh['member'=16,'band'=32] {'member','band'}, use_global_device_ids=true, to_apply=%region_20.21 | all-reduce | flops 1 | bytes 8 | tf_op jit(solution)/shard_map/psum | solution.py:117
  647.9 1.4 fusion.92
  (145 shorter events, 29.7 us)
Async XLA Ops:
  7.2 32.8 %copy-start = (f32[16,16]{1,0:T(8,128)S(1)}, f32[16,16]{1,0:T(8,128)}, u32[]{:S(2)}) copy-start(f32[16,16]{1,0:T(8,128)} %param.11) | copy-start | bytes 3076
  7.2 160.8 %all-reduce.4.cloned.1.call-start = ((), (), s32[]{:S(2)}) async-start(), calls=%async_computation | async-start | bytes 1572864 | tf_op jit(solution)/shard_map/psum | solution.py:107
  12.9 158.4 %copy-start.25 = (s32[516]{0:T(1024)}, s32[516]{0:T(1024)S(1)}, u32[]{:S(2)}) copy-start(s32[516]{0:T(1024)S(1)} %iota_add_fusion) | copy-start | bytes 6196
  14.2 6.6 collective-permute-start
  18.2 6.4 collective-permute-start.1
  19.6 17.9 %copy-start.4 = (f32[16]{0:T(128)}, f32[16]{0:T(128)S(1)}, u32[]{:S(2)}) copy-start(f32[16]{0:T(128)S(1)} %get-tuple-element.60) | copy-start | bytes 196
  19.6 17.9 %copy-start.7 = (f32[16]{0:T(128)}, f32[16]{0:T(128)S(1)}, u32[]{:S(2)}) copy-start(f32[16]{0:T(128)S(1)} %get-tuple-element.61) | copy-start | bytes 196
  19.6 17.9 %copy-start.10 = (f32[16]{0:T(128)}, f32[16]{0:T(128)S(1)}, u32[]{:S(2)}) copy-start(f32[16]{0:T(128)S(1)} %get-tuple-element.62) | copy-start | bytes 196
  19.6 17.9 %copy-start.13 = (f32[16]{0:T(128)}, f32[16]{0:T(128)S(1)}, u32[]{:S(2)}) copy-start(f32[16]{0:T(128)S(1)} %get-tuple-element.63) | copy-start | bytes 196
  19.6 17.9 %copy-start.16 = (f32[16]{0:T(128)}, f32[16]{0:T(128)S(1)}, u32[]{:S(2)}) copy-start(f32[16]{0:T(128)S(1)} %get-tuple-element.64) | copy-start | bytes 196
  19.6 17.9 %copy-start.19 = (f32[16]{0:T(128)}, f32[16]{0:T(128)S(1)}, u32[]{:S(2)}) copy-start(f32[16]{0:T(128)S(1)} %get-tuple-element.65) | copy-start | bytes 196
  19.6 17.9 %copy-start.22 = (f32[16]{0:T(128)}, f32[16]{0:T(128)S(1)}, u32[]{:S(2)}) copy-start(f32[16]{0:T(128)S(1)} %get-tuple-element.66) | copy-start | bytes 196
  26.7 6.6 %collective-permute-start.2 = (bf16[1,16,4,1440]{3,1,2,0:T(8,128)(2,1)S(1)}, bf16[1,16,4,1440]{3,1,2,0:T(8,128)(2,1)S(1)}, u32[]{:S(2)}, u32[]{:S(2)}) collective-permute-start(bf16[1,16,4,1440]{3,1,2,0:T(8,128)(2,1)S(1)} %convert_element_type.392), channel_id=1, source_target_pairs={{0,1},{1,2},{2,3},{3,4},{4,5},{5,6},{6,7},{7,8},{8,9},{9,10},{10,1... | collective-permute-start | bytes 552968 | tf_op jit(solution)/shard_map/ppermute | solution.py:20
  31.0 6.4 collective-permute-start.3
  39.9 485.6 %all-reduce.6.cloned.1.call-start = ((), (), s32[]{:S(2)}) async-start(), calls=%async_computation.1 | async-start | bytes 1572864 | tf_op jit(solution)/shard_map/psum | solution.py:107
  172.6 7.1 %collective-permute-start.4 = (bf16[1,16,4,1440]{3,1,2,0:T(8,128)(2,1)S(1)}, bf16[1,16,4,1440]{3,1,2,0:T(8,128)(2,1)S(1)}, u32[]{:S(2)}, u32[]{:S(2)}) collective-permute-start(bf16[1,16,4,1440]{3,1,2,0:T(8,128)(2,1)S(1)} %convert_element_type.405), channel_id=1, source_target_pairs={{0,1},{1,2},{2,3},{3,4},{4,5},{5,6},{6,7},{7,8},{8,9},{9,10},{10,1... | collective-permute-start | bytes 552968 | tf_op jit(solution)/shard_map/ppermute | solution.py:20
  175.7 7.3 %collective-permute-start.5 = (bf16[1,16,4,1440]{3,1,2,0:T(8,128)(2,1)S(1)}, bf16[1,16,4,1440]{3,1,2,0:T(8,128)(2,1)}, u32[]{:S(2)}, u32[]{:S(2)}) collective-permute-start(bf16[1,16,4,1440]{3,1,2,0:T(8,128)(2,1)S(1)} %convert_element_type.405), channel_id=1, source_target_pairs={{1,0},{2,1},{3,2},{4,3},{5,4},{6,5},{7,6},{8,7},{9,8},{10,9},{11,1... | collective-permute-start | bytes 552968 | tf_op jit(solution)/shard_map/ppermute | solution.py:23
  394.0 11.1 %copy-start.5 = (f32[16]{0:T(128)S(1)}, f32[16]{0:T(128)}, u32[]{:S(2)}) copy-start(f32[16]{0:T(128)} %copy-done.4) | copy-start | bytes 196
  394.0 11.1 %copy-start.8 = (f32[16]{0:T(128)S(1)}, f32[16]{0:T(128)}, u32[]{:S(2)}) copy-start(f32[16]{0:T(128)} %copy-done.7) | copy-start | bytes 196
  394.0 11.1 %copy-start.11 = (f32[16]{0:T(128)S(1)}, f32[16]{0:T(128)}, u32[]{:S(2)}) copy-start(f32[16]{0:T(128)} %copy-done.10) | copy-start | bytes 196
  394.0 11.1 %copy-start.14 = (f32[16]{0:T(128)S(1)}, f32[16]{0:T(128)}, u32[]{:S(2)}) copy-start(f32[16]{0:T(128)} %copy-done.13) | copy-start | bytes 196
  394.0 11.1 %copy-start.17 = (f32[16]{0:T(128)S(1)}, f32[16]{0:T(128)}, u32[]{:S(2)}) copy-start(f32[16]{0:T(128)} %copy-done.16) | copy-start | bytes 196
  394.0 11.1 %copy-start.20 = (f32[16]{0:T(128)S(1)}, f32[16]{0:T(128)}, u32[]{:S(2)}) copy-start(f32[16]{0:T(128)} %copy-done.19) | copy-start | bytes 196
  394.0 11.1 %copy-start.23 = (f32[16]{0:T(128)S(1)}, f32[16]{0:T(128)}, u32[]{:S(2)}) copy-start(f32[16]{0:T(128)} %copy-done.22) | copy-start | bytes 196
  394.0 7.2 %collective-permute-start.6 = (bf16[1,16,4,1440]{3,1,2,0:T(8,128)(2,1)S(1)}, bf16[1,16,4,1440]{3,1,2,0:T(8,128)(2,1)S(1)}, u32[]{:S(2)}, u32[]{:S(2)}) collective-permute-start(bf16[1,16,4,1440]{3,1,2,0:T(8,128)(2,1)S(1)} %convert_element_type.417), channel_id=1, source_target_pairs={{0,1},{1,2},{2,3},{3,4},{4,5},{5,6},{6,7},{7,8},{8,9},{9,10},{10,1... | collective-permute-start | bytes 552968 | tf_op jit(solution)/shard_map/ppermute | solution.py:20
  397.7 7.4 %collective-permute-start.7 = (bf16[1,16,4,1440]{3,1,2,0:T(8,128)(2,1)S(1)}, bf16[1,16,4,1440]{3,1,2,0:T(8,128)(2,1)S(1)}, u32[]{:S(2)}, u32[]{:S(2)}) collective-permute-start(bf16[1,16,4,1440]{3,1,2,0:T(8,128)(2,1)S(1)} %convert_element_type.417), channel_id=1, source_target_pairs={{1,0},{2,1},{3,2},{4,3},{5,4},{6,5},{7,6},{8,7},{9,8},{10,9},{11,1... | collective-permute-start | bytes 552968 | tf_op jit(solution)/shard_map/ppermute | solution.py:23
  531.2 6.5 collective-permute-start.8
  534.3 7.3 %collective-permute-start.9 = (bf16[1,16,4,1440]{3,1,2,0:T(8,128)(2,1)S(1)}, bf16[1,16,4,1440]{3,1,2,0:T(8,128)(2,1)}, u32[]{:S(2)}, u32[]{:S(2)}) collective-permute-start(bf16[1,16,4,1440]{3,1,2,0:T(8,128)(2,1)S(1)} %convert_element_type.430), channel_id=1, source_target_pairs={{1,0},{2,1},{3,2},{4,3},{5,4},{6,5},{7,6},{8,7},{9,8},{10,9},{11,1... | collective-permute-start | bytes 552968 | tf_op jit(solution)/shard_map/ppermute | solution.py:23
  536.9 5.8 copy-start.15
  536.9 5.8 copy-start.18
  536.9 5.8 copy-start.21
  536.9 5.8 copy-start.24
  (9 other events, 33.3 us)
Sparse Core Ops, SparseCore 0:
  40.1 127.9 all-reduce.3
  407.7 117.7 all-reduce.5
where the time goes:
time: 659 us; the launch traced here: 658 us
  blocking collectives  298 us (45%)
  waiting for transfers between devices  266 us (40%)
  between operations  24.5 us (4%)
  starting transfers between devices  24.4 us (4%)
  other arithmetic  23.4 us (4%)
  local copies, waits for them, and re-layouts  13.4 us (2%)
  matrix products  8.49 us (1%)
    psum x2, waiting for transfers between devices, shards(): summed = lax.psum(partial_image, 'member')  243 us
    psum x2, blocking collectives, shards(): lax.psum(local_dot(res_members, res_members, res_static, res_static, grou...  196 us
    psum x1, blocking collectives, shards(): lax.psum(local_dot(dir_members, hes_members, dir_static, hes_static, grou...  101 us
    ppermute x5, waiting for transfers between devices, with_halo(): lax.ppermute(lax.slice_in_dim(block, 0, width, axis=dim), axis, backward)  18.7 us
    ppermute x5, starting transfers between devices, with_halo(): lax.ppermute(lax.slice_in_dim(block, block.shape[dim] - width, None, axis...  17.9 us
  transfers between devices with their start and end apart: 12, of which 11 were waited for; matrix products, arithmetic and copies ran while one was open for 1% of the time, Pallas kernels for 0%

commit v1 on v0

--- a/solution.py
+++ b/solution.py
@@ -115,7 +115,8 @@
             image,
         )
         curvature = lax.psum(
-            local_dot(dir_members, hes_members, dir_static, hes_static, groups), ("member", "band")
+            lax.psum(local_dot(dir_members, hes_members, dir_static, hes_static, groups), "band"),
+            "member",
         )
         alpha = norm_now / curvature
         sol_members = sol_members + alpha * dir_members

time: 659 us -> 757 us (1.15)
  blocking collectives: 298 us -> 392 us
    psum x0 -> x2, blocking collectives: none -> 78.9 us  [shards(): lax.psum(lax.psum(local_dot(dir_members, hes_members, dir_static, hes_sta...]
    psum x1 -> x2, blocking collectives: 101 us -> 118 us  [shards(): lax.psum(local_dot(dir_members, hes_members, dir_static, hes_static, grou...]
  transfers between devices with their start and end apart: 12 -> 12, of which waited for: 11 -> 12; matrix products, arithmetic and copies ran while one was open for 1% -> 1% of each run, Pallas kernels for 0% -> 0%
where the time goes in v1:
time: 757 us; the launch traced here: 753 us
  blocking collectives  392 us (52%)
  waiting for transfers between devices  268 us (35%)
  between operations  24.9 us (3%)
  starting transfers between devices  23.6 us (3%)
  other arithmetic  23.3 us (3%)
  local copies, waits for them, and re-layouts  13.1 us (2%)
  matrix products  8.43 us (1%)
    psum x2, waiting for transfers between devices, shards(): summed = lax.psum(partial_image, 'member')  244 us
    psum x2, blocking collectives, shards(): lax.psum(local_dot(res_members, res_members, res_static, res_static, grou...  194 us
    psum x2, blocking collectives, shards(): lax.psum(local_dot(dir_members, hes_members, dir_static, hes_static, grou...  118 us
    psum x2, blocking collectives, shards(): lax.psum(lax.psum(local_dot(dir_members, hes_members, dir_static, hes_sta...  78.9 us
    ppermute x5, waiting for transfers between devices, with_halo(): lax.ppermute(lax.slice_in_dim(block, 0, width, axis=dim), axis, backward)  19.2 us
    ppermute x5, starting transfers between devices, with_halo(): lax.ppermute(lax.slice_in_dim(block, block.shape[dim] - width, None, axis...  17.1 us
  transfers between devices with their start and end apart: 12, of which 12 were waited for; matrix products, arithmetic and copies ran while one was open for 1% of the time, Pallas kernels for 0%

profile of v1, /device:TPU:1, one launch (start us, length us, event | category | flops | bytes accessed | tf_op | source)
XLA Modules:
  0.0 752.8 jit_solution(3407091323659355581)
XLA Ops:
  10.1 1.6 fusion.13
  14.2 4.0 collective-permute-start
  18.2 1.3 collective-permute-start.1
  20.8 3.8 collective-permute-done.1
  26.7 4.0 collective-permute-start.2
  33.3 4.1 collective-permute-done.3
  38.1 1.8 fusion.10
  41.3 126.9 %all-reduce.3.cloned.1.call-done = f32[2,16,4,1440]{3,2,1,0:T(4,128)} async-done(((f32[2,16,4,1440]{3,2,1,0:T(4,128)}), f32[2,16,4,1440]{3,2,1,0:T(4,128)}) %all-reduce.3.cloned.1.call-update) | async-done | bytes 737296 | tf_op jit(solution)/shard_map/psum | solution.py:107
  168.2 1.7 multiply_reduce_fusion.1
  170.3 1.4 fusion.46
  174.3 3.1 collective-permute-start.4
  177.4 1.3 collective-permute-start.5
  178.7 1.3 fusion.42
  180.9 3.9 collective-permute-done.5
  185.7 2.1 multiply_reduce_fusion.4
  189.1 59.2 %psum.58 = f32[]{:T(128)} all-reduce(f32[]{:T(128)S(6)} %add.242), channel_id=1, replica_groups=mesh['member'=16,'band'=32] {'band'}, use_global_device_ids=true, to_apply=%region_11.12 | all-reduce | flops 1 | bytes 8 | tf_op jit(solution)/shard_map/psum | solution.py:118
  248.9 39.5 %psum.59 = f32[]{:T(128)} all-reduce(f32[]{:T(128)} %psum.58), channel_id=1, replica_groups=mesh['member'=16,'band'=32] {'member'}, use_global_device_ids=true, to_apply=%region_12.13 | all-reduce | flops 1 | bytes 8 | tf_op jit(solution)/shard_map/psum | solution.py:117
  288.4 99.5 %psum.56 = f32[]{:T(128)} all-reduce(f32[]{:T(128)S(6)} %add.221), channel_id=1, replica_groups=mesh['member'=16,'band'=32] {'member','band'}, use_global_device_ids=true, to_apply=%region_5.6 | all-reduce | flops 1 | bytes 8 | tf_op jit(solution)/shard_map/psum | solution.py:98
  392.2 94.8 %psum.60 = f32[]{:T(128)} all-reduce(f32[]{:T(128)S(6)} %add.243), channel_id=1, replica_groups=mesh['member'=16,'band'=32] {'member','band'}, use_global_device_ids=true, to_apply=%region_15.16 | all-reduce | flops 1 | bytes 8 | tf_op jit(solution)/shard_map/psum | solution.py:128
  493.5 2.8 collective-permute-start.6
  496.3 1.3 collective-permute-start.7
  497.6 2.2 collective-permute-done.6
  499.9 3.8 collective-permute-done.7
  504.4 1.8 fusion.12
  507.7 116.9 %all-reduce.5.cloned.1.call-done = f32[2,16,4,1440]{3,2,1,0:T(4,128)} async-done(((f32[2,16,4,1440]{3,2,1,0:T(4,128)}), f32[2,16,4,1440]{3,2,1,0:T(4,128)}) %all-reduce.5.cloned.1.call-update) | async-done | bytes 737296 | tf_op jit(solution)/shard_map/psum | solution.py:107
  624.7 1.8 multiply_reduce_fusion
  630.1 3.1 collective-permute-start.8
  633.2 1.3 collective-permute-start.9
  636.6 3.8 collective-permute-done.9
  642.2 59.3 %psum.62 = f32[]{:T(128)} all-reduce(f32[]{:T(128)S(6)} %add.266), channel_id=1, replica_groups=mesh['member'=16,'band'=32] {'band'}, use_global_device_ids=true, to_apply=%region_21.22 | all-reduce | flops 1 | bytes 8 | tf_op jit(solution)/shard_map/psum | solution.py:118
  701.5 39.4 %psum.63 = f32[]{:T(128)} all-reduce(f32[]{:T(128)} %psum.62), channel_id=1, replica_groups=mesh['member'=16,'band'=32] {'member'}, use_global_device_ids=true, to_apply=%region_22.23 | all-reduce | flops 1 | bytes 8 | tf_op jit(solution)/shard_map/psum | solution.py:117
  742.2 1.4 fusion.92
  (148 shorter events, 33.9 us)
Async XLA Ops:
  7.2 32.8 %copy-start = (f32[16,16]{1,0:T(8,128)S(1)}, f32[16,16]{1,0:T(8,128)}, u32[]{:S(2)}) copy-start(f32[16,16]{1,0:T(8,128)} %param.11) | copy-start | bytes 3076
  7.2 161.0 %all-reduce.3.cloned.1.call-start = ((), (), s32[]{:S(2)}) async-start(), calls=%async_computation | async-start | bytes 1572864 | tf_op jit(solution)/shard_map/psum | solution.py:107
  12.9 160.2 %copy-start.25 = (s32[516]{0:T(1024)}, s32[516]{0:T(1024)S(1)}, u32[]{:S(2)}) copy-start(s32[516]{0:T(1024)S(1)} %iota_add_fusion) | copy-start | bytes 6196
  13.8 5.7 copy-start.28
  14.2 6.6 collective-permute-start
  18.2 6.4 collective-permute-start.1
  19.6 17.9 %copy-start.4 = (f32[16]{0:T(128)}, f32[16]{0:T(128)S(1)}, u32[]{:S(2)}) copy-start(f32[16]{0:T(128)S(1)} %get-tuple-element.58) | copy-start | bytes 196
  19.6 17.9 %copy-start.7 = (f32[16]{0:T(128)}, f32[16]{0:T(128)S(1)}, u32[]{:S(2)}) copy-start(f32[16]{0:T(128)S(1)} %get-tuple-element.59) | copy-start | bytes 196
  19.6 17.9 %copy-start.10 = (f32[16]{0:T(128)}, f32[16]{0:T(128)S(1)}, u32[]{:S(2)}) copy-start(f32[16]{0:T(128)S(1)} %get-tuple-element.60) | copy-start | bytes 196
  19.6 17.9 %copy-start.13 = (f32[16]{0:T(128)}, f32[16]{0:T(128)S(1)}, u32[]{:S(2)}) copy-start(f32[16]{0:T(128)S(1)} %get-tuple-element.61) | copy-start | bytes 196
  19.6 17.9 %copy-start.16 = (f32[16]{0:T(128)}, f32[16]{0:T(128)S(1)}, u32[]{:S(2)}) copy-start(f32[16]{0:T(128)S(1)} %get-tuple-element.62) | copy-start | bytes 196
  19.6 17.9 %copy-start.19 = (f32[16]{0:T(128)}, f32[16]{0:T(128)S(1)}, u32[]{:S(2)}) copy-start(f32[16]{0:T(128)S(1)} %get-tuple-element.63) | copy-start | bytes 196
  19.6 17.9 %copy-start.22 = (f32[16]{0:T(128)}, f32[16]{0:T(128)S(1)}, u32[]{:S(2)}) copy-start(f32[16]{0:T(128)S(1)} %get-tuple-element.64) | copy-start | bytes 196
  26.7 6.6 collective-permute-start.2
  31.0 6.4 collective-permute-start.3
  39.9 584.7 %all-reduce.5.cloned.1.call-start = ((), (), s32[]{:S(2)}) async-start(), calls=%async_computation.1 | async-start | bytes 1572864 | tf_op jit(solution)/shard_map/psum | solution.py:107
  174.3 6.5 collective-permute-start.4
  177.4 7.3 collective-permute-start.5
  493.4 10.3 %copy-start.5 = (f32[16]{0:T(128)S(1)}, f32[16]{0:T(128)}, u32[]{:S(2)}) copy-start(f32[16]{0:T(128)} %copy-done.4) | copy-start | bytes 196
  493.4 10.3 %copy-start.8 = (f32[16]{0:T(128)S(1)}, f32[16]{0:T(128)}, u32[]{:S(2)}) copy-start(f32[16]{0:T(128)} %copy-done.7) | copy-start | bytes 196
  493.4 10.3 %copy-start.11 = (f32[16]{0:T(128)S(1)}, f32[16]{0:T(128)}, u32[]{:S(2)}) copy-start(f32[16]{0:T(128)} %copy-done.10) | copy-start | bytes 196
  493.4 10.3 %copy-start.14 = (f32[16]{0:T(128)S(1)}, f32[16]{0:T(128)}, u32[]{:S(2)}) copy-start(f32[16]{0:T(128)} %copy-done.13) | copy-start | bytes 196
  493.4 10.3 %copy-start.17 = (f32[16]{0:T(128)S(1)}, f32[16]{0:T(128)}, u32[]{:S(2)}) copy-start(f32[16]{0:T(128)} %copy-done.16) | copy-start | bytes 196
  493.5 10.3 %copy-start.20 = (f32[16]{0:T(128)S(1)}, f32[16]{0:T(128)}, u32[]{:S(2)}) copy-start(f32[16]{0:T(128)} %copy-done.19) | copy-start | bytes 196
  493.5 10.3 %copy-start.23 = (f32[16]{0:T(128)S(1)}, f32[16]{0:T(128)}, u32[]{:S(2)}) copy-start(f32[16]{0:T(128)} %copy-done.22) | copy-start | bytes 196
  493.5 6.4 collective-permute-start.6
  496.3 7.4 collective-permute-start.7
  630.1 6.5 collective-permute-start.8
  633.2 7.2 collective-permute-start.9
  635.7 4.7 copy-start.18
  635.7 4.7 copy-start.21
  635.7 4.7 copy-start.24
  (9 other events, 29.2 us)
Sparse Core Ops, SparseCore 0:
  40.1 128.0 all-reduce.2
  506.3 118.2 all-reduce.4
